TPU v7x, 32 devices: a whole 2x2x4 slice. The times are simulated.
32 devices in a mesh: gx: 2 (over core), gy: 4 (over y, x), gz: 4 (over z).
Axes of the slice: x: 2, y: 2, z: 4, core: 2. Of those that a mesh axis runs over, the one named last changes fastest.
Arguments:
- displacement_start: float32 [3, 8, 64, 512], P(None, 'gx', 'gy', 'gz'), may hold values from -4 to 4
- external_force: float32 [3, 8, 64, 512], P(None, 'gx', 'gy', 'gz'), may hold values from -6 to 6
- damage_old: float32 [8, 64, 512], P('gx', 'gy', 'gz'), may hold values from 0 to 0.9
- history_old: float32 [8, 64, 512], P('gx', 'gy', 'gz'), may hold values from 0.02 to 2
- crack_labels: int32 [8, 64, 512], P('gx', 'gy', 'gz'), may hold values 0 or 1
- fixed_flags: int32 [8, 64, 512], P('gx', 'gy', 'gz'), may hold values 0 or 1
Outputs:
- displacement: float32 [3, 8, 64, 512], P(None, 'gx', 'gy', 'gz')
- damage: float32 [8, 64, 512], P('gx', 'gy', 'gz')
- history: float32 [8, 64, 512], P('gx', 'gy', 'gz')
All inputs are finite; a program needn't handle non-finite values. No bound on the sum of `crack_labels` or of `fixed_flags` on one device may be relied on, other than what follows from the above.
Results may differ from a plain program's by a relative error of at most 0.0001.
Values sent between devices are 32-bit elements; how exact they have to be, the bound alone decides.
A program may use at most 64 MiB of HBM per device.

v0:
```python
import functools
import jax
import jax.numpy as jnp
import numpy as np
from jax import lax
from jax.experimental import pallas as pl
from jax.experimental.pallas import tpu as pltpu
from jax.sharding import PartitionSpec as P

DISP_ITERS = 4
DMG_ITERS = 2


LAME_LAMBDA = 0.5769230769230769
LAME_MU = 0.38461538461538464
BULK_MODULUS = LAME_LAMBDA + 2.0 * LAME_MU / 3.0
RESIDUAL_STIFFNESS = 0.001
TOUGHNESS = 1.0
LENGTH_SCALE = 2.0
CRACK_HISTORY = 40.0


def padded_2(cells, sides, width):
    for axis, dim in sides:
        count = lax.axis_size(axis)
        ends = count - 1
        head = lax.slice_in_dim(cells, 0, width, axis=dim)
        tail = lax.slice_in_dim(cells, cells.shape[dim] - width, cells.shape[dim], axis=dim)
        cells = jnp.concatenate(
            [
                lax.ppermute(tail, axis, [(i, (i + 1) % count) for i in range(ends)]),
                cells,
                lax.ppermute(head, axis, [((i + 1) % count, i) for i in range(ends)]),
            ],
            axis=dim,
        )
    return cells


def corner_offsets(corner):
    return (corner >> 2 & 1, corner >> 1 & 1, corner & 1)


def shape_gradients(sample):
    gradient = np.zeros((3, 8))
    for corner in range(8):
        offsets = corner_offsets(corner)
        values = [sample[k] if offsets[k] else 1.0 - sample[k] for k in range(3)]
        slopes = [1.0 if offsets[k] else -1.0 for k in range(3)]
        gradient[0, corner] = slopes[0] * values[1] * values[2]
        gradient[1, corner] = values[0] * slopes[1] * values[2]
        gradient[2, corner] = values[0] * values[1] * slopes[2]
    return gradient


def strain_matrix(gradient):
    strain = np.zeros((6, 24))
    for corner in range(8):
        column = 3 * corner
        strain[0, column] = gradient[0, corner]
        strain[1, column + 1] = gradient[1, corner]
        strain[2, column + 2] = gradient[2, corner]
        strain[3, column] = gradient[1, corner]
        strain[3, column + 1] = gradient[0, corner]
        strain[4, column + 1] = gradient[2, corner]
        strain[4, column + 2] = gradient[1, corner]
        strain[5, column] = gradient[2, corner]
        strain[5, column + 2] = gradient[0, corner]
    return strain


def element_tables():
    moduli = np.zeros((6, 6))
    moduli[:3, :3] = LAME_LAMBDA
    for k in range(3):
        moduli[k, k] += 2.0 * LAME_MU
        moduli[k + 3, k + 3] = LAME_MU
    points = [0.5 - 0.5 / np.sqrt(3.0), 0.5 + 0.5 / np.sqrt(3.0)]
    stiff_table = np.zeros((24, 24))
    laplace_table = np.zeros((8, 8))
    for sample_index in range(8):
        sample = tuple((points[k] for k in corner_offsets(sample_index)))
        gradient = shape_gradients(sample)
        strain = strain_matrix(gradient)
        stiff_table += 0.125 * strain.T @ moduli @ strain
        laplace_table += 0.125 * gradient.T @ gradient
    centre_table = strain_matrix(shape_gradients((0.5, 0.5, 0.5)))
    return (
        stiff_table.astype(np.float32),
        laplace_table.astype(np.float32),
        centre_table.astype(np.float32),
    )


def corner_views(padded, element_shape):
    corner_list = []
    for corner in range(8):
        offx, offy, offz = corner_offsets(corner)
        corner_list.append(
            padded[
                ...,
                offx : offx + element_shape[0],
                offy : offy + element_shape[1],
                offz : offz + element_shape[2],
            ]
        )
    return corner_list


def assemble_nodes(pieces):
    running = None
    for corner in range(8):
        offx, offy, offz = corner_offsets(corner)
        leading = [(0, 0)] * (pieces[corner].ndim - 3)
        placed = jnp.pad(
            pieces[corner], leading + [(offx, 1 - offx), (offy, 1 - offy), (offz, 1 - offz)]
        )
        running = placed if running is None else running + placed
    return running


def line_valid(position, devices, count):
    index = position * count + jnp.arange(count + 1, dtype=jnp.int32) - 1
    return ((index >= 0) & (index <= devices * count - 2)).astype(jnp.float32)


def strain_energy(strain):
    trace = strain[0] + strain[1] + strain[2]
    deviator = strain[:3] - trace[None] / 3.0
    shear = strain[3:]
    tensile = jnp.maximum(trace, 0.0)
    return 0.5 * BULK_MODULUS * tensile * tensile + LAME_MU * (
        jnp.sum(deviator * deviator, axis=0) + 0.5 * jnp.sum(shear * shear, axis=0)
    )


def forces_to_nodes(forces, stiffness):
    pieces = [stiffness[None] * forces[3 * target : 3 * target + 3] for target in range(8)]
    return assemble_nodes(pieces)


def element_apply(padded, stiffness, stiff_table):
    element_shape = stiffness.shape
    flat = jnp.stack(corner_views(padded, element_shape)).reshape(24, -1)
    forces = jnp.dot(stiff_table, flat, precision=lax.Precision.HIGHEST).reshape(
        (24,) + element_shape
    )
    return forces_to_nodes(forces, stiffness)


def laplace_apply(padded, element_valid, laplace_table):
    element_shape = element_valid.shape
    flat = jnp.stack(corner_views(padded, element_shape)).reshape(8, -1)
    forces = jnp.dot(laplace_table, flat, precision=lax.Precision.HIGHEST).reshape(
        (8,) + element_shape
    )
    return assemble_nodes([element_valid * forces[target] for target in range(8)])


def single_pair(pair):
    return tuple(lax.psum(pair, ("gx", "gy", "gz")))


def conjugate(solutions, residuals, inverses, counts, apply_fn):
    solutions = list(solutions)
    residuals = list(residuals)
    number = len(solutions)
    steps = max(counts)

    def pair_totals(pairs):
        return [single_pair(pairs[0])]

    precs = [inverses[0] * residuals[0]]
    applied = apply_fn(precs, list(range(number)))
    pairs = pair_totals([(jnp.sum(residuals[0] * precs[0]), jnp.sum(precs[0] * applied[0]))])
    norms = [pair[0] for pair in pairs]
    lengths = [pair[0] / pair[1] for pair in pairs]
    directions = list(precs)
    alongs = list(applied)
    for step in range(steps):
        active = [i for i in range(number) if step < counts[i]]
        for i in active:
            solutions[i] = solutions[i] + lengths[i] * directions[i]
            residuals[i] = residuals[i] - lengths[i] * alongs[i]
        later = [i for i in active if step + 1 < counts[i]]
        if later:
            i = later[0]
            precs[i] = inverses[i] * residuals[i]
            images = apply_fn([precs[i] for i in later], later)
            pairs = pair_totals(
                [
                    (jnp.sum(residuals[i] * precs[i]), jnp.sum(precs[i] * images[k]))
                    for k, i in enumerate(later)
                ]
            )
            for k, i in enumerate(later):
                norm_next, curve_sum = pairs[k]
                ratio = norm_next / norms[i]
                lengths[i] = norm_next / (curve_sum - ratio * norm_next / lengths[i])
                directions[i] = precs[i] + ratio * directions[i]
                alongs[i] = images[k] + ratio * alongs[i]
                norms[i] = norm_next
    return solutions


def body_any_mesh(displacement_start, external_force, damage_old, history_old, crack_labels, fixed_flags):
    tables = element_tables()
    stiff_table = jnp.asarray(tables[0], jnp.float32)
    laplace_table = jnp.asarray(tables[1], jnp.float32)
    centre_table = jnp.asarray(tables[2], jnp.float32)
    highest = lax.Precision.HIGHEST
    size_x, size_y, size_z = damage_old.shape
    free_mask = 1.0 - fixed_flags.astype(jnp.float32)
    start_disp = displacement_start * free_mask[None]
    element_valid = (
        line_valid(lax.axis_index("gx"), lax.axis_size("gx"), size_x)[:, None, None]
        * line_valid(lax.axis_index("gy"), lax.axis_size("gy"), size_y)[None, :, None]
        * line_valid(lax.axis_index("gz"), lax.axis_size("gz"), size_z)[None, None, :]
    )
    element_shape = element_valid.shape
    start_pad = padded_2(
        jnp.concatenate([start_disp, damage_old[None]], axis=0),
        (("gx", 1), ("gy", 2), ("gz", 3)),
        1,
    )
    corner_list = corner_views(start_pad, element_shape)
    damage_mean = sum((view[3] for view in corner_list)) / 8.0
    stiffness = ((1.0 - damage_mean) ** 2 + RESIDUAL_STIFFNESS) * element_valid
    flat = jnp.stack([view[:3] for view in corner_list]).reshape(24, -1)
    combined = jnp.dot(
        jnp.concatenate([stiff_table, centre_table], axis=0), flat, precision=highest
    )
    forces = combined[:24].reshape((24,) + element_shape)
    strain = combined[24:].reshape((6,) + element_shape)
    start_image = forces_to_nodes(forces, stiffness)[:, 1:-1, 1:-1, 1:-1]
    energy = strain_energy(strain) * element_valid
    nodal_energy = assemble_nodes([energy] * 8)[1:-1, 1:-1, 1:-1] / 8.0
    history = jnp.maximum(
        jnp.maximum(history_old, nodal_energy), CRACK_HISTORY * crack_labels.astype(jnp.float32)
    )
    stiff_diag = jnp.diagonal(stiff_table)
    diag_pieces = [
        stiffness[None] * stiff_diag[3 * target : 3 * target + 3][:, None, None, None]
        for target in range(8)
    ]
    elastic_diag = assemble_nodes(diag_pieces)[:, 1:-1, 1:-1, 1:-1]
    inverse_elastic = 1.0 / (free_mask[None] * elastic_diag + (1.0 - free_mask[None]))

    def constrained(nodal_field):
        masked = free_mask[None] * nodal_field
        padded = padded_2(masked, (("gx", 1), ("gy", 2), ("gz", 3)), 1)
        nodes = element_apply(padded, stiffness, stiff_table)[:, 1:-1, 1:-1, 1:-1]
        return free_mask[None] * nodes + (1.0 - free_mask[None]) * nodal_field

    reaction = TOUGHNESS / LENGTH_SCALE + 2.0 * history
    laplace_diag = assemble_nodes(
        [element_valid * laplace_table[target, target] for target in range(8)]
    )[1:-1, 1:-1, 1:-1]
    inverse_damage = 1.0 / (TOUGHNESS * LENGTH_SCALE * laplace_diag + reaction)
    residual = free_mask[None] * (external_force - start_image)
    start_lap = laplace_apply(start_pad[3], element_valid, laplace_table)[1:-1, 1:-1, 1:-1]
    damage_residual = 2.0 * history - (TOUGHNESS * LENGTH_SCALE * start_lap + reaction * damage_old)

    def damage_operator(nodal_field):
        padded = padded_2(nodal_field, (("gx", 0), ("gy", 1), ("gz", 2)), 1)
        lap_nodes = laplace_apply(padded, element_valid, laplace_table)[1:-1, 1:-1, 1:-1]
        return TOUGHNESS * LENGTH_SCALE * lap_nodes + reaction * nodal_field

    def single_elastic(fields, active):
        return [constrained(fields[0])]

    def single_damage(fields, active):
        return [damage_operator(fields[0])]

    displacement = conjugate(
        [start_disp], [residual], [inverse_elastic], [DISP_ITERS], single_elastic
    )[0]
    damage = conjugate(
        [damage_old], [damage_residual], [inverse_damage], [DMG_ITERS], single_damage
    )[0]
    return (displacement, damage, history)


DEPTH = 8
SPECTRUM = 3.2
MESH = pl.DeviceIdType.MESH


def walsh_tables():
    stiff, laplace, _ = element_tables()
    signs = np.array(
        [
            [np.prod([1.0 if c >> k & 1 else (-1.0 if m >> k & 1 else 1.0) for k in range(3)]) for c in range(8)]
            for m in range(8)
        ]
    )
    wide = np.kron(signs, np.eye(3))
    stiff_modes = wide @ stiff.astype(np.float64) @ wide.T / 64.0
    laplace_modes = signs @ laplace.astype(np.float64) @ signs.T / 64.0
    return stiff_modes, laplace_modes, float(stiff[0, 0]), float(laplace[0, 0])


def kernel(
    sizes,
    disp_ref,
    force_ref,
    damage_ref,
    history_ref,
    labels_ref,
    flags_ref,
    out_disp,
    out_damage,
    out_history,
    ext,
    modes,
    basis,
    resid,
    stiff,
    inverse,
    hist,
    dbasis,
    dresid,
    zsend,
    zrecv,
    zpart,
    sums,
    ysend_sem,
    yrecv_sem,
    zsend_sem,
    zrecv_sem,
    xsend_sem,
    xrecv_sem,
    asend_sem,
    arecv_sem,
):
    ngy, ngz, lx, ly, lz = sizes
    nx = 2 * lx
    rows, lanes = ly + 2 * DEPTH, lz + 128
    fields = 8
    npeer = ngy * ngz
    stiff_modes, laplace_modes, stiff_diag, laplace_diag = walsh_tables()
    gx, gy, gz = lax.axis_index("gx"), lax.axis_index("gy"), lax.axis_index("gz")
    xo = gx * lx
    other = 1 - gx
    me = gy * ngz + gz
    partner = (other, gy, gz)

    for p in range(lx):
        flag = flags_ref[p].astype(jnp.float32)
        free = 1.0 - flag
        for c in range(3):
            ext[c, xo + p, 0:ly, 0:lz] = free * disp_ref[c, p]
            ext[3 + c, xo + p, 0:ly, 0:lz] = force_ref[c, p]
        ext[6, xo + p, 0:ly, 0:lz] = damage_ref[p]
        top = jnp.maximum(history_ref[p], CRACK_HISTORY * labels_ref[p].astype(jnp.float32))
        ext[7, xo + p, 0:ly, 0:lz] = top * (free - flag)
        for f in range(fields):
            ext[f, xo + p, ly:rows, 0:lz] = jnp.zeros((2 * DEPTH, lz), jnp.float32)
    zrecv[...] = jnp.zeros_like(zrecv)

    barrier = pltpu.get_barrier_semaphore()
    pl.semaphore_signal(barrier, inc=1, device_id=partner, device_id_type=MESH)
    for o in range(1, npeer):
        q = lax.rem(me + o, npeer)
        pl.semaphore_signal(barrier, inc=1, device_id=(gx, q // ngz, lax.rem(q, ngz)), device_id_type=MESH)
    pl.semaphore_wait(barrier, npeer)

    own = pl.ds(xo, lx)

    def xcopy(src, dst, k):
        return pltpu.make_async_remote_copy(
            src_ref=src, dst_ref=dst, send_sem=xsend_sem.at[k], recv_sem=xrecv_sem.at[k],
            device_id=partner, device_id_type=MESH,
        )

    def ycopy(src_row, dst_row, k, shift):
        return pltpu.make_async_remote_copy(
            src_ref=ext.at[:, own, src_row : src_row + DEPTH, 0:lz],
            dst_ref=ext.at[:, own, dst_row : dst_row + DEPTH, 0:lz],
            send_sem=ysend_sem.at[k], recv_sem=yrecv_sem.at[k],
            device_id=(gx, gy + shift, gz), device_id_type=MESH,
        )

    def zcopy(k, shift):
        return pltpu.make_async_remote_copy(
            src_ref=zsend.at[k], dst_ref=zrecv.at[k],
            send_sem=zsend_sem.at[k], recv_sem=zrecv_sem.at[k],
            device_id=(gx, gy, gz + shift), device_id_type=MESH,
        )

    has_down, has_up = gy > 0, gy < ngy - 1
    has_left, has_right = gz > 0, gz < ngz - 1
    y_down = ycopy(0, ly, 0, -1)
    y_up = ycopy(ly - DEPTH, ly + DEPTH, 1, 1)
    x_own = xcopy(ext.at[:, own, 0:ly, 0:lz], ext.at[:, own, 0:ly, 0:lz], 0)
    pl.when(has_down)(y_down.start)
    pl.when(has_up)(y_up.start)
    x_own.start()
    pl.when(has_up)(y_down.wait_recv)
    pl.when(has_down)(y_up.wait_recv)

    x_ghost = xcopy(ext.at[:, own, ly:rows, 0:lz], ext.at[:, own, ly:rows, 0:lz], 1)
    x_ghost.start()
    group = lax.broadcasted_iota(jnp.int32, (rows, 128), 1) // 8
    count = fields * lx
    for j in range(count // 16):
        low = jnp.zeros((rows, 128), jnp.float32)
        high = jnp.zeros((rows, 128), jnp.float32)
        for k in range(16):
            f, p = divmod(16 * j + k, lx)
            first = ext[f, xo + p, :, 0:128]
            if lz == 128:
                turned = pltpu.roll(first, (8 * k + 8) % 128, 1) if k < 15 else first
                low = jnp.where(group == (k + 1) % 16, turned, low)
                high = jnp.where(group == k, turned, high)
        zsend[0, j] = low
        zsend[1, j] = high
    z_left = zcopy(0, -1)
    z_right = zcopy(1, 1)
    pl.when(has_left)(z_left.start)
    pl.when(has_right)(z_right.start)
    pl.when(has_right)(z_left.wait_recv)
    pl.when(has_left)(z_right.wait_recv)
    x_z = xcopy(zrecv, zpart, 2)
    x_z.start()

    def unpack(source, base):
        for j in range(count // 16):
            low = source[0, j]
            high = source[1, j]
            for k in range(16):
                f, p = divmod(16 * j + k, lx)
                both = jnp.where(group == k, high, jnp.where(group == (k + 1) % 16, low, 0.0))
                ext[f, base + p, :, lz : lz + 128] = (
                    pltpu.roll(both, (120 - 8 * k) % 128, 1) if k < 15 else both
                )

    unpack(zrecv, xo)
    x_own.wait_recv()
    x_ghost.wait_recv()
    x_z.wait_recv()
    unpack(zpart, other * lx)

    row = lax.broadcasted_iota(jnp.int32, (rows, lanes), 0)
    lane = lax.broadcasted_iota(jnp.int32, (rows, lanes), 1)
    ypos = gy * ly + jnp.where(row < ly + DEPTH, row, row - rows)
    zpos = gz * lz + jnp.where(lane < lz + 64, lane, lane - lanes)
    valid = jnp.where(
        (ypos >= 0) & (ypos <= ngy * ly - 2) & (zpos >= 0) & (zpos <= ngz * lz - 2), 1.0, 0.0
    )

    def up(a, axis):
        return pltpu.roll(a, a.shape[axis] - 1, axis)

    def down(a, axis):
        return pltpu.roll(a, 1, axis)

    def forward(u):
        near = up(u, 1)
        zs, zd = u + near, near - u
        a, b = up(zs, 0), up(zd, 0)
        return zs + a, a - zs, zd + b, b - zd

    def backward(ss, yd, zd, yz):
        s = (ss - yd) + down(ss + yd, 0)
        d = (zd - yz) + down(zd + yz, 0)
        return (s - d) + down(s + d, 1)

    def total8(a):
        s = a + up(a, 1)
        return s + up(s, 0)

    def total8_back(a):
        s = a + down(a, 1)
        return s + down(s, 0)

    def damage_sum(p):
        return total8(ext[6, p])

    def g_body(p, low):
        high = damage_sum(p + 1)
        rest = 1.0 - (low + high) * 0.125
        stiff[p] = (rest * rest + RESIDUAL_STIFFNESS) * valid
        return high

    lax.fori_loop(0, nx - 1, g_body, damage_sum(0))
    stiff[nx - 1] = jnp.zeros((rows, lanes), jnp.float32)

    def inv_body(p, low):
        here = total8_back(stiff[p])
        q = stiff_diag * (low + here)
        free = ext[7, p] > 0.0
        inverse[p] = jnp.where(free, 1.0 / jnp.where(free, q, 1.0), 0.0)
        return here

    lax.fori_loop(0, nx, inv_body, jnp.zeros((rows, lanes), jnp.float32))

    def pass_one(load, number):
        def step(p, carry):
            for c in range(number):
                out = forward(load(c, p))
                for m in range(4):
                    modes[4 * c + m, p] = out[m]
            return carry

        lax.fori_loop(0, nx, step, 0)

    def sm(mode_a, comp_a, mode_b, comp_b):
        return float(stiff_modes[3 * mode_a + comp_a, 3 * mode_b + comp_b])

    k_lame = sm(4, 0, 2, 1)
    k_two = sm(4, 0, 4, 0) - k_lame
    k_shear = sm(2, 0, 2, 0)
    k_twist = sm(3, 0, 5, 1)
    k_bend = sm(3, 1, 3, 1)
    k_cross = sm(3, 1, 5, 0)
    k_last = sm(7, 0, 7, 0)

    def element_pass(with_energy):
        def step(chunk, carry):
            r = pl.ds(pl.multiple_of(chunk * 8, 8), 8)
            low = [modes[m, 0, r, :] for m in range(12)]
            held = [None] * 12
            for p in range(nx):
                acc = held
                if p < nx - 1:
                    high = [modes[m, p + 1, r, :] for m in range(12)]
                    S = [low[m] + high[m] if m % 4 else None for m in range(12)]
                    D = [high[m] - low[m] for m in range(12)]
                    g = stiff[p, r, :]
                    xX, xXY, xXZ, xXYZ = D[0:4]
                    yX, yXY, yXZ, yXYZ = D[4:8]
                    zX, zXY, zXZ, zXYZ = D[8:12]
                    _, xY, xZ, xYZ = S[0:4]
                    _, yY, yZ, yYZ = S[4:8]
                    _, zY, zZ, zYZ = S[8:12]
                    div = xX + yY + zZ
                    sxy, sxz, syz = xY + yX, xZ + zX, yZ + zY
                    if with_energy:
                        trace = 0.25 * div
                        tens = jnp.maximum(trace, 0.0)
                        third = trace / 3.0
                        ex, ey, ez = 0.25 * xX - third, 0.25 * yY - third, 0.25 * zZ - third
                        dev = ex * ex + ey * ey + ez * ez
                        she = (sxy * sxy + sxz * sxz + syz * syz) * 0.0625
                        energy = 0.5 * BULK_MODULUS * tens * tens + LAME_MU * (dev + 0.5 * she)
                        hist[p, r, :] = jnp.where(g > 0.0, energy, 0.0)
                    gl, g2, gs = k_lame * g, k_two * g, k_shear * g
                    gt, gb, gc, g3 = k_twist * g, k_bend * g, k_cross * g, k_last * g
                    pressure = gl * div
                    fxX, fyY, fzZ = pressure + g2 * xX, pressure + g2 * yY, pressure + g2 * zZ
                    txy, txz, tyz = gs * sxy, gs * sxz, gs * syz
                    tw = xYZ + yXZ + zXY
                    fxYZ, fyXZ, fzXY = gt * (xYZ + tw), gt * (yXZ + tw), gt * (zXY + tw)
                    fyYZ, fxXZ = gb * yYZ + gc * xXZ, gb * xXZ + gc * yYZ
                    fzYZ, fxXY = gb * zYZ + gc * xXY, gb * xXY + gc * zYZ
                    fyXY, fzXZ = gb * yXY + gc * zXZ, gb * zXZ + gc * yXY
                    FD = [
                        fxX, fxXY, fxXZ, g3 * xXYZ,
                        txy, fyXY, fyXZ, g3 * yXYZ,
                        txz, fzXY, fzXZ, g3 * zXYZ,
                    ]
                    FS = [
                        None, txy, txz, fxYZ,
                        None, fyY, tyz, fyYZ,
                        None, tyz, fzZ, fzYZ,
                    ]
                    acc = [(-FD[m]) if FS[m] is None else FS[m] - FD[m] for m in range(12)]
                    if p:
                        acc = [acc[m] + held[m] for m in range(12)]
                    held = [FD[m] if FS[m] is None else FS[m] + FD[m] for m in range(12)]
                    low = high
                for m in range(12):
                    modes[m, p, r, :] = acc[m]
            return carry

        lax.fori_loop(0, rows // 8, step, 0)

    def nodes(c, p):
        return backward(*(modes[4 * c + m, p] for m in range(4)))

    def fold(a):
        part = a[0:8, 0:128]
        for i in range(0, ly, 8):
            for k in range(0, lz, 128):
                if i or k:
                    part = part + a[i : i + 8, k : k + 128]
        return part

    zero = jnp.zeros((8, 128), jnp.float32)
    inner = (slice(0, ly), slice(0, lz))

    pass_one(lambda c, p: ext[c, p], 3)
    element_pass(True)

    def start_step(p, carry):
        dot = carry
        inv = inverse[p]
        for c in range(3):
            r = ext[3 + c, p] - nodes(c, p)
            v = inv * r
            basis[c, p] = v
            resid[c, p] = r[inner]
            dot = dot + fold((v * r)[inner])
        return dot

    vector = [lax.fori_loop(0, nx, start_step, zero)]
    hist[nx - 1] = jnp.zeros((rows, lanes), jnp.float32)

    def hist_step(p, low):
        here = total8_back(hist[p])
        hist[p] = jnp.maximum(jnp.abs(ext[7, p]), 0.125 * (low + here))
        return here

    lax.fori_loop(0, nx, hist_step, jnp.zeros((rows, lanes), jnp.float32))

    gram = []
    for k in range(DISP_ITERS):
        pass_one(lambda c, p, k=k: basis[3 * k + c, p], 3)
        element_pass(False)
        more = k + 1 < DISP_ITERS

        def apply_step(p, carry, k=k, more=more):
            carry = list(carry)
            inv = inverse[p] * (2.0 / SPECTRUM) if more else None
            for c in range(3):
                w = nodes(c, p)
                wi = w[inner]
                for j in range(k + 1):
                    carry[j] = carry[j] + fold(basis[3 * j + c, p, 0:ly, 0:lz] * wi)
                if more:
                    v = inv * w - basis[3 * k + c, p]
                    if k:
                        v = 2.0 * v - basis[3 * (k - 1) + c, p] + 0.0
                    basis[3 * (k + 1) + c, p] = v
                    carry[k + 1] = carry[k + 1] + fold(v[inner] * resid[c, p])
            return tuple(carry)

        got = lax.fori_loop(0, nx, apply_step, (zero,) * (k + 1 + (1 if more else 0)))
        gram.append(list(got[: k + 1]))
        if more:
            vector.append(got[k + 1])

    l_one = float(laplace_modes[1, 1]) * TOUGHNESS * LENGTH_SCALE
    l_two = float(laplace_modes[3, 3]) * TOUGHNESS * LENGTH_SCALE
    l_three = float(laplace_modes[7, 7]) * TOUGHNESS * LENGTH_SCALE
    validrow = ((ypos >= 0) & (ypos <= ngy * ly - 2) & (zpos >= 0) & (zpos <= ngz * lz - 2))

    def laplace_pass(load):
        def prime(p):
            return forward(load(p))

        def step(p, carry):
            low, held = carry[:4], carry[4:]
            high = forward(load(p + 1))
            D = [high[m] - low[m] for m in range(4)]
            S = [low[m] + high[m] for m in range(1, 4)]
            F = [l_one * D[0], l_two * D[1], l_two * D[2], l_three * D[3]]
            F = [jnp.where(validrow, f, 0.0) for f in F]
            T = [l_one * S[0], l_one * S[1], l_two * S[2]]
            T = [jnp.where(validrow, f, 0.0) for f in T]
            acc = [-F[0], T[0] - F[1], T[1] - F[2], T[2] - F[3]]
            for m in range(4):
                modes[m, p] = acc[m] + held[m]
            return tuple(high) + (F[0], T[0] + F[1], T[1] + F[2], T[2] + F[3])

        blank = jnp.zeros((rows, lanes), jnp.float32)
        out = lax.fori_loop(0, nx - 1, step, tuple(prime(0)) + (blank,) * 4)
        for m in range(4):
            modes[m, nx - 1] = out[4 + m]

    corners = total8_back(valid) * (laplace_diag * TOUGHNESS * LENGTH_SCALE)

    def reaction_of(p):
        return TOUGHNESS / LENGTH_SCALE + 2.0 * hist[p]

    def damage_inverse(p):
        twice = jnp.where((p > 0) & (p < nx - 1), 2.0, 1.0)
        return 1.0 / (corners * twice + reaction_of(p))

    laplace_pass(lambda p: ext[6, p])

    def dstart(p, dot):
        d = ext[6, p]
        r = 2.0 * hist[p] - (nodes(0, p) + reaction_of(p) * d)
        v = damage_inverse(p) * r
        dbasis[0, p] = v
        dresid[p] = r[inner]
        return dot + fold((v * r)[inner])

    dvector = [lax.fori_loop(0, nx, dstart, zero)]
    dgram = []
    for k in range(DMG_ITERS):
        laplace_pass(lambda p, k=k: dbasis[k, p])
        more = k + 1 < DMG_ITERS

        def dstep(p, carry, k=k, more=more):
            carry = list(carry)
            here = dbasis[k, p]
            w = nodes(0, p) + reaction_of(p) * here
            for j in range(k + 1):
                carry[j] = carry[j] + fold((dbasis[j, p] * w)[inner])
            if more:
                v = damage_inverse(p) * w - here
                if k:
                    v = 2.0 * v - dbasis[k - 1, p]
                dbasis[k + 1, p] = v
                carry[k + 1] = carry[k + 1] + fold(v[inner] * dresid[p])
            return tuple(carry)

        got = lax.fori_loop(0, nx, dstep, (zero,) * (k + 1 + (1 if more else 0)))
        dgram.append(list(got[: k + 1]))
        if more:
            dvector.append(got[k + 1])

    parts = vector + dvector + [x for g in gram for x in g] + [x for g in dgram for x in g]
    at = lax.broadcasted_iota(jnp.int32, (8, 128), 1)
    packed = zero
    for i, part in enumerate(parts):
        packed = jnp.where(at == i, jnp.sum(jnp.sum(part, axis=0, keepdims=True), axis=1, keepdims=True), packed)
    sums[me] = packed

    def peer_copy(o, slot):
        q = lax.rem(me + o, npeer)
        return pltpu.make_async_remote_copy(
            src_ref=sums.at[me], dst_ref=sums.at[slot],
            send_sem=asend_sem.at[o - 1], recv_sem=arecv_sem.at[o - 1],
            device_id=(gx, q // ngz, lax.rem(q, ngz)), device_id_type=MESH,
        )

    sends = [peer_copy(o, me) for o in range(1, npeer)]
    for s in sends:
        s.start()
    for p in range(lx):
        out_history[p] = hist[xo + p, 0:ly, 0:lz]
    for o in range(1, npeer):
        peer_copy(o, lax.rem(me + npeer - o, npeer)).wait_recv()
    whole = sums[0]
    for i in range(1, npeer):
        whole = whole + sums[i]

    values = [
        jnp.sum(jnp.where(at[0:1] == i, whole[0:1], 0.0), axis=1, keepdims=True)
        for i in range(len(parts))
    ]
    nd, ng = DISP_ITERS, DMG_ITERS

    def solve(rhs, lower):
        n = len(rhs)
        A = [[lower[max(i, j)][min(i, j)] for j in range(n)] for i in range(n)]
        b = list(rhs)
        for i in range(n):
            pivot = 1.0 / A[i][i]
            for r in range(i + 1, n):
                ratio = A[r][i] * pivot
                for c in range(i + 1, n):
                    A[r][c] = A[r][c] - ratio * A[i][c]
                b[r] = b[r] - ratio * b[i]
        out = [None] * n
        for i in reversed(range(n)):
            s = b[i]
            for j in range(i + 1, n):
                s = s - A[i][j] * out[j]
            out[i] = s / A[i][i]
        return out

    def triangle(flat, n):
        return [[flat[k * (k + 1) // 2 + j] for j in range(k + 1)] for k in range(n)]

    rest = values[nd + ng :]
    cut = nd * (nd + 1) // 2
    weights = solve(values[:nd], triangle(rest[:cut], nd))
    dweights = solve(values[nd : nd + ng], triangle(rest[cut:], ng))
    for p in range(lx):
        for c in range(3):
            x = ext[c, xo + p, 0:ly, 0:lz]
            for k in range(nd):
                x = x + weights[k] * basis[3 * k + c, xo + p, 0:ly, 0:lz]
            out_disp[c, p] = x
        d = ext[6, xo + p, 0:ly, 0:lz]
        for k in range(ng):
            d = d + dweights[k] * dbasis[k, xo + p, 0:ly, 0:lz]
        out_damage[p] = d

    pl.when(has_down)(y_down.wait_send)
    pl.when(has_up)(y_up.wait_send)
    pl.when(has_left)(z_left.wait_send)
    pl.when(has_right)(z_right.wait_send)
    x_own.wait_send()
    x_ghost.wait_send()
    x_z.wait_send()
    for s in sends:
        s.wait_send()


def body_fused(sizes, *arrays):
    ngy, ngz, lx, ly, lz = sizes
    nx, rows, lanes, fields = 2 * lx, ly + 2 * DEPTH, lz + 128, 8
    packs = fields * lx // 16
    npeer = ngy * ngz
    f32 = jnp.float32
    wide = (nx, rows, lanes)
    vmem = pl.BlockSpec(memory_space=pltpu.VMEM)
    dma = pltpu.SemaphoreType.DMA
    return pl.pallas_call(
        functools.partial(kernel, sizes),
        out_shape=(
            jax.ShapeDtypeStruct((3, lx, ly, lz), f32),
            jax.ShapeDtypeStruct((lx, ly, lz), f32),
            jax.ShapeDtypeStruct((lx, ly, lz), f32),
        ),
        in_specs=[vmem] * 6,
        out_specs=(vmem,) * 3,
        scratch_shapes=[
            pltpu.VMEM((fields,) + wide, f32),
            pltpu.VMEM((12,) + wide, f32),
            pltpu.VMEM((3 * DISP_ITERS,) + wide, f32),
            pltpu.VMEM((3, nx, ly, lz), f32),
            pltpu.VMEM(wide, f32),
            pltpu.VMEM(wide, f32),
            pltpu.VMEM(wide, f32),
            pltpu.VMEM((DMG_ITERS,) + wide, f32),
            pltpu.VMEM((nx, ly, lz), f32),
            pltpu.VMEM((2, packs, rows, 128), f32),
            pltpu.VMEM((2, packs, rows, 128), f32),
            pltpu.VMEM((2, packs, rows, 128), f32),
            pltpu.VMEM((npeer, 8, 128), f32),
            dma((2,)),
            dma((2,)),
            dma((2,)),
            dma((2,)),
            dma((3,)),
            dma((3,)),
            dma((npeer - 1,)),
            dma((npeer - 1,)),
        ],
        compiler_params=pltpu.CompilerParams(
            collective_id=0, has_side_effects=True, vmem_limit_bytes=60 * 1024 * 1024
        ),
    )(*arrays)


def solution(mesh):
    shape = dict(mesh.shape)

    def body(*arrays):
        lx, ly, lz = arrays[2].shape
        fits = shape["gx"] == 2 and shape["gy"] * shape["gz"] > 1
        fits = fits and lx % 2 == 0 and ly % 8 == 0 and lz == 128
        if fits:
            return body_fused((shape["gy"], shape["gz"], lx, ly, lz), *arrays)
        return body_any_mesh(*arrays)

    return jax.shard_map(
        body,
        mesh=mesh,
        in_specs=(
            P(None, "gx", "gy", "gz"),
            P(None, "gx", "gy", "gz"),
            P("gx", "gy", "gz"),
            P("gx", "gy", "gz"),
            P("gx", "gy", "gz"),
            P("gx", "gy", "gz"),
        ),
        out_specs=(P(None, "gx", "gy", "gz"), P("gx", "gy", "gz"), P("gx", "gy", "gz")),
        check_vma=False,
    )
```

profile of v0, /device:TPU:0, one launch (start us, length us, event | category | flops | bytes accessed | tf_op | source)
XLA Modules:
  0.0 49.2 jit_solution(18261621971941469019)
XLA Ops:
  0.6 45.6 %shard_map.85 = (f32[3,4,16,128]{3,2,1,0:T(8,128)}, f32[4,16,128]{2,1,0:T(8,128)}, f32[4,16,128]{2,1,0:T(8,128)}) custom-call(f32[3,4,16,128]{3,2,1,0:T(8,128)} %disp_ref.1, f32[3,4,16,128]{3,2,1,0:T(8,128)} %force_ref.1, f32[4,16,128]{2,1,0:T(8,128)} %damage_ref.1, f32[4,16,128]{2,1,0:T(8,128)} %history_ref.1, s32[4,16,128]{2,1,0:T(8,128)} %labels_ref.1, ...), custom_call_target="tpu_custom_call" | custom-call | tf_op jit(solution)/shard_map/pallas_call | solution.py:805
  46.2 0.0 copy-start.1
  46.3 1.5 %copy.12 = f32[3,4,16,128]{3,2,1,0:T(8,128)} copy(f32[3,4,16,128]{3,2,1,0:T(8,128)} %get-tuple-element.6) | data formatting | bytes 196608
  47.8 0.0 copy-done.1
  47.8 0.0 copy-start
  47.8 0.6 %copy.13 = f32[4,16,128]{2,1,0:T(8,128)} copy(f32[4,16,128]{2,1,0:T(8,128)S(1)} %copy-done.1) | data formatting | bytes 65536
  48.4 0.2 copy-done
  48.6 0.6 %copy.14 = f32[4,16,128]{2,1,0:T(8,128)} copy(f32[4,16,128]{2,1,0:T(8,128)S(1)} %copy-done) | data formatting | bytes 65536
Async XLA Ops:
  46.2 1.6 %copy-start.1 = (f32[4,16,128]{2,1,0:T(8,128)S(1)}, f32[4,16,128]{2,1,0:T(8,128)}, u32[]{:S(2)}) copy-start(f32[4,16,128]{2,1,0:T(8,128)} %get-tuple-element.7) | copy-start | bytes 98308
  47.8 0.8 %copy-start = (f32[4,16,128]{2,1,0:T(8,128)S(1)}, f32[4,16,128]{2,1,0:T(8,128)}, u32[]{:S(2)}) copy-start(f32[4,16,128]{2,1,0:T(8,128)} %get-tuple-element.8) | copy-start | bytes 98308
where the time goes:
time: 49.4 us; the launch traced here: 49.2 us
  Pallas kernels  45.6 us (92%)
  local copies, waits for them, and re-layouts  2.93 us (6%)
  between operations  0.65 us (1%)
    pallas_call x1, Pallas kernels, body_fused(): pl.pallas_call(functools.partial(kernel, sizes), out_shape=(jax.ShapeDtyp...  45.6 us
    unnamed x7, local copies, waits for them, and re-layouts  2.93 us

commit v1 on v0

--- a/solution.py
+++ b/solution.py
@@ -318,6 +318,9 @@
     stiff,
     inverse,
     hist,
+    react,
+    spread,
+    dinverse,
     dbasis,
     dresid,
     zsend,
@@ -335,9 +338,10 @@
 ):
     ngy, ngz, lx, ly, lz = sizes
     nx = 2 * lx
-    rows, lanes = ly + 2 * DEPTH, lz + 128
+    rows = ly + 2 * DEPTH
     fields = 8
     npeer = ngy * ngz
+    count = fields * lx
     stiff_modes, laplace_modes, stiff_diag, laplace_diag = walsh_tables()
     gx, gy, gz = lax.axis_index("gx"), lax.axis_index("gy"), lax.axis_index("gz")
     xo = gx * lx
@@ -345,24 +349,22 @@
     me = gy * ngz + gz
     partner = (other, gy, gz)
 
-    for p in range(lx):
-        flag = flags_ref[p].astype(jnp.float32)
-        free = 1.0 - flag
-        for c in range(3):
-            ext[c, xo + p, 0:ly, 0:lz] = free * disp_ref[c, p]
-            ext[3 + c, xo + p, 0:ly, 0:lz] = force_ref[c, p]
-        ext[6, xo + p, 0:ly, 0:lz] = damage_ref[p]
-        top = jnp.maximum(history_ref[p], CRACK_HISTORY * labels_ref[p].astype(jnp.float32))
-        ext[7, xo + p, 0:ly, 0:lz] = top * (free - flag)
-        for f in range(fields):
-            ext[f, xo + p, ly:rows, 0:lz] = jnp.zeros((2 * DEPTH, lz), jnp.float32)
-    zrecv[...] = jnp.zeros_like(zrecv)
-
+    GZ = nx
     barrier = pltpu.get_barrier_semaphore()
     pl.semaphore_signal(barrier, inc=1, device_id=partner, device_id_type=MESH)
     for o in range(1, npeer):
         q = lax.rem(me + o, npeer)
         pl.semaphore_signal(barrier, inc=1, device_id=(gx, q // ngz, lax.rem(q, ngz)), device_id_type=MESH)
+
+    for p in range(lx):
+        flag = flags_ref[p].astype(jnp.float32)
+        free = 1.0 - flag
+        for c in range(3):
+            ext[c, xo + p, 0:ly] = free * disp_ref[c, p]
+            ext[3 + c, xo + p, 0:ly] = force_ref[c, p]
+        ext[6, xo + p, 0:ly] = damage_ref[p]
+        top = jnp.maximum(history_ref[p], CRACK_HISTORY * labels_ref[p].astype(jnp.float32))
+        ext[7, xo + p, 0:ly] = top * (free - flag)
     pl.semaphore_wait(barrier, npeer)
 
     own = pl.ds(xo, lx)
@@ -390,29 +392,48 @@
 
     has_down, has_up = gy > 0, gy < ngy - 1
     has_left, has_right = gz > 0, gz < ngz - 1
-    y_down = ycopy(0, ly, 0, -1)
-    y_up = ycopy(ly - DEPTH, ly + DEPTH, 1, 1)
+    send_down = ycopy(0, ly, 0, -1)
+    send_up = ycopy(ly - DEPTH, ly + DEPTH, 1, 1)
     x_own = xcopy(ext.at[:, own, 0:ly, 0:lz], ext.at[:, own, 0:ly, 0:lz], 0)
-    pl.when(has_down)(y_down.start)
-    pl.when(has_up)(y_up.start)
+    pl.when(has_down)(send_down.start)
+    pl.when(has_up)(send_up.start)
     x_own.start()
-    pl.when(has_up)(y_down.wait_recv)
-    pl.when(has_down)(y_up.wait_recv)
+
+    @pl.when(jnp.logical_not(has_up))
+    def _():
+        for p in range(lx):
+            for f in range(fields):
+                ext[f, xo + p, ly : ly + DEPTH] = jnp.zeros((DEPTH, lz), jnp.float32)
+
+    @pl.when(jnp.logical_not(has_down))
+    def _():
+        for p in range(lx):
+            for f in range(fields):
+                ext[f, xo + p, ly + DEPTH : rows] = jnp.zeros((DEPTH, lz), jnp.float32)
+
+    @pl.when(jnp.logical_not(has_right))
+    def _():
+        zrecv[0] = jnp.zeros((count // 16, rows, 128), jnp.float32)
+
+    @pl.when(jnp.logical_not(has_left))
+    def _():
+        zrecv[1] = jnp.zeros((count // 16, rows, 128), jnp.float32)
+
+    pl.when(has_up)(send_down.wait_recv)
+    pl.when(has_down)(send_up.wait_recv)
 
     x_ghost = xcopy(ext.at[:, own, ly:rows, 0:lz], ext.at[:, own, ly:rows, 0:lz], 1)
     x_ghost.start()
     group = lax.broadcasted_iota(jnp.int32, (rows, 128), 1) // 8
-    count = fields * lx
     for j in range(count // 16):
         low = jnp.zeros((rows, 128), jnp.float32)
         high = jnp.zeros((rows, 128), jnp.float32)
         for k in range(16):
             f, p = divmod(16 * j + k, lx)
             first = ext[f, xo + p, :, 0:128]
-            if lz == 128:
-                turned = pltpu.roll(first, (8 * k + 8) % 128, 1) if k < 15 else first
-                low = jnp.where(group == (k + 1) % 16, turned, low)
-                high = jnp.where(group == k, turned, high)
+            turned = pltpu.roll(first, (8 * k + 8) % 128, 1) if k < 15 else first
+            low = jnp.where(group == (k + 1) % 16, turned, low)
+            high = jnp.where(group == k, turned, high)
         zsend[0, j] = low
         zsend[1, j] = high
     z_left = zcopy(0, -1)
@@ -424,86 +445,137 @@
     x_z = xcopy(zrecv, zpart, 2)
     x_z.start()
 
-    def unpack(source, base):
-        for j in range(count // 16):
-            low = source[0, j]
-            high = source[1, j]
-            for k in range(16):
-                f, p = divmod(16 * j + k, lx)
-                both = jnp.where(group == k, high, jnp.where(group == (k + 1) % 16, low, 0.0))
-                ext[f, base + p, :, lz : lz + 128] = (
-                    pltpu.roll(both, (120 - 8 * k) % 128, 1) if k < 15 else both
-                )
-
-    unpack(zrecv, xo)
+    def unpack(source, base, into, field):
+        j = field * lx // 16
+        low = source[0, j]
+        high = source[1, j]
+        for p in range(lx):
+            k = field * lx + p - 16 * j
+            both = jnp.where(group == k, high, low)
+            turned = pltpu.roll(both, lax.rem(16 * base + (16 * p - 8 * k) % 128, 128), 1)
+            into = jnp.where(group // 2 == base + p, turned, into)
+        return into
+
+    blank = jnp.zeros((rows, 128), jnp.float32)
+    half = [unpack(zrecv, xo, blank, f) for f in range(fields)]
+    for f in range(fields):
+        ext[f, GZ] = half[f]
     x_own.wait_recv()
     x_ghost.wait_recv()
     x_z.wait_recv()
-    unpack(zpart, other * lx)
-
-    row = lax.broadcasted_iota(jnp.int32, (rows, lanes), 0)
-    lane = lax.broadcasted_iota(jnp.int32, (rows, lanes), 1)
+    for f in range(fields):
+        ext[f, GZ] = unpack(zpart, other * lx, ext[f, GZ], f)
+
+    row = lax.broadcasted_iota(jnp.int32, (rows, 128), 0)
+    lane = lax.broadcasted_iota(jnp.int32, (rows, 128), 1)
+    inside = lane % 16
     ypos = gy * ly + jnp.where(row < ly + DEPTH, row, row - rows)
-    zpos = gz * lz + jnp.where(lane < lz + 64, lane, lane - lanes)
-    valid = jnp.where(
-        (ypos >= 0) & (ypos <= ngy * ly - 2) & (zpos >= 0) & (zpos <= ngz * lz - 2), 1.0, 0.0
-    )
-
-    def up(a, axis):
-        return pltpu.roll(a, a.shape[axis] - 1, axis)
-
-    def down(a, axis):
-        return pltpu.roll(a, 1, axis)
-
-    def forward(u):
-        near = up(u, 1)
+    zpos = gz * lz + lane
+    zghost = gz * lz + jnp.where(inside < 8, inside - 8, inside + (lz - 8))
+    yvalid = (ypos >= 0) & (ypos <= ngy * ly - 2)
+    valid = jnp.where(yvalid & (zpos <= ngz * lz - 2), 1.0, 0.0)
+    gvalid = jnp.where(
+        yvalid & (zghost >= 0) & (zghost <= ngz * lz - 2) & (lane < 16 * (nx - 1)), 1.0, 0.0
+    )
+
+    def y_up(a):
+        return pltpu.roll(a, rows - 1, 0)
+
+    def y_dn(a):
+        return pltpu.roll(a, 1, 0)
+
+    def z_up(a, ghost, p):
+        return jnp.where(lane == 127, pltpu.roll(ghost, 119 - 16 * p, 1), pltpu.roll(a, 127, 1))
+
+    def z_up_take(acc, a, p):
+        return jnp.where(lane == 16 * p + 7, pltpu.roll(a, 16 * p + 7, 1), acc)
+
+    def z_dn(a, ghost, p):
+        return jnp.where(lane == 0, pltpu.roll(ghost, 121 - 16 * p, 1), pltpu.roll(a, 1, 1))
+
+    def z_dn_take(acc, a, p):
+        return jnp.where(lane == 16 * p + 8, pltpu.roll(a, 16 * p + 9, 1), acc)
+
+    def x_up(a):
+        return pltpu.roll(a, 112, 1)
+
+    def x_dn(a):
+        return pltpu.roll(a, 16, 1)
+
+    def forward(u, near):
         zs, zd = u + near, near - u
-        a, b = up(zs, 0), up(zd, 0)
+        a, b = y_up(zs), y_up(zd)
         return zs + a, a - zs, zd + b, b - zd
 
-    def backward(ss, yd, zd, yz):
-        s = (ss - yd) + down(ss + yd, 0)
-        d = (zd - yz) + down(zd + yz, 0)
-        return (s - d) + down(s + d, 1)
-
-    def total8(a):
-        s = a + up(a, 1)
-        return s + up(s, 0)
-
-    def total8_back(a):
-        s = a + down(a, 1)
-        return s + down(s, 0)
+    def half_back(ss, yd, zd, yz):
+        s = (ss - yd) + y_dn(ss + yd)
+        d = (zd - yz) + y_dn(zd + yz)
+        return s - d, s + d
 
     def damage_sum(p):
-        return total8(ext[6, p])
-
-    def g_body(p, low):
-        high = damage_sum(p + 1)
+        a = ext[6, p]
+        s = a + z_up(a, ext[6, GZ], p)
+        return s + y_up(s), a
+
+    def rigidity(low, high, mask):
         rest = 1.0 - (low + high) * 0.125
-        stiff[p] = (rest * rest + RESIDUAL_STIFFNESS) * valid
-        return high
-
-    lax.fori_loop(0, nx - 1, g_body, damage_sum(0))
-    stiff[nx - 1] = jnp.zeros((rows, lanes), jnp.float32)
-
-    def inv_body(p, low):
-        here = total8_back(stiff[p])
-        q = stiff_diag * (low + here)
+        return (rest * rest + RESIDUAL_STIFFNESS) * mask
+
+    def g_body(p, carry):
+        low, ghost = carry
+        high, a = damage_sum(p + 1)
+        stiff[p] = rigidity(low, high, valid)
+        return high, z_up_take(ghost, a, p + 1)
+
+    sum_first, a_first = damage_sum(0)
+    g_ghost = z_up_take(pltpu.roll(ext[6, GZ], 127, 1), a_first, 0)
+    _, g_ghost = lax.fori_loop(0, nx - 1, g_body, (sum_first, g_ghost), unroll=True)
+    g_ghost = ext[6, GZ] + g_ghost
+    g_ghost = g_ghost + y_up(g_ghost)
+    stiff[GZ] = rigidity(g_ghost, x_up(g_ghost), gvalid)
+    stiff[nx - 1] = blank
+
+    def gather_back(ref, emit):
+        ghost = ref[GZ]
+
+        def step(p, carry):
+            low, taken = carry
+            a = ref[p]
+            s = a + z_dn(a, ghost, p)
+            here = s + y_dn(s)
+            emit(p, low + here)
+            return here, z_dn_take(taken, a, p)
+
+        _, taken = lax.fori_loop(0, nx, step, (blank, pltpu.roll(ghost, 1, 1)), unroll=True)
+        s = ghost + taken
+        s = s + y_dn(s)
+        emit(GZ, s + x_dn(s))
+
+    def inv_emit(p, total):
+        q = stiff_diag * total
         free = ext[7, p] > 0.0
         inverse[p] = jnp.where(free, 1.0 / jnp.where(free, q, 1.0), 0.0)
-        return here
-
-    lax.fori_loop(0, nx, inv_body, jnp.zeros((rows, lanes), jnp.float32))
+
+    gather_back(stiff, inv_emit)
 
     def pass_one(load, number):
-        def step(p, carry):
+        ghosts = [load(c, GZ) for c in range(number)]
+
+        def step(p, taken):
+            new = []
             for c in range(number):
-                out = forward(load(c, p))
+                u = load(c, p)
+                out = forward(u, z_up(u, ghosts[c], p))
                 for m in range(4):
                     modes[4 * c + m, p] = out[m]
-            return carry
-
-        lax.fori_loop(0, nx, step, 0)
+                new.append(z_up_take(taken[c], u, p))
+            return tuple(new)
+
+        taken = lax.fori_loop(0, nx, step, tuple(pltpu.roll(g, 127, 1) for g in ghosts), unroll=True)
+        for c in range(number):
+            out = forward(ghosts[c], taken[c])
+            for m in range(4):
+                modes[4 * c + m, GZ] = out[m]
 
     def sm(mode_a, comp_a, mode_b, comp_b):
         return float(stiff_modes[3 * mode_a + comp_a, 3 * mode_b + comp_b])
@@ -517,67 +589,86 @@
     k_last = sm(7, 0, 7, 0)
 
     def element_pass(with_energy):
+        def element(low, high, g, p, r):
+            S = [low[m] + high[m] if m % 4 else None for m in range(12)]
+            D = [high[m] - low[m] for m in range(12)]
+            xX, xXY, xXZ, xXYZ = D[0:4]
+            yX, yXY, yXZ, yXYZ = D[4:8]
+            zX, zXY, zXZ, zXYZ = D[8:12]
+            _, xY, xZ, xYZ = S[0:4]
+            _, yY, yZ, yYZ = S[4:8]
+            _, zY, zZ, zYZ = S[8:12]
+            div = xX + yY + zZ
+            sxy, sxz, syz = xY + yX, xZ + zX, yZ + zY
+            if with_energy:
+                trace = 0.25 * div
+                tens = jnp.maximum(trace, 0.0)
+                third = trace / 3.0
+                ex, ey, ez = 0.25 * xX - third, 0.25 * yY - third, 0.25 * zZ - third
+                dev = ex * ex + ey * ey + ez * ez
+                she = (sxy * sxy + sxz * sxz + syz * syz) * 0.0625
+                energy = 0.5 * BULK_MODULUS * tens * tens + LAME_MU * (dev + 0.5 * she)
+                hist[p, r, :] = jnp.where(g > 0.0, energy, 0.0)
+            gl, g2, gs = k_lame * g, k_two * g, k_shear * g
+            gt, gb, gc, g3 = k_twist * g, k_bend * g, k_cross * g, k_last * g
+            pressure = gl * div
+            fxX, fyY, fzZ = pressure + g2 * xX, pressure + g2 * yY, pressure + g2 * zZ
+            txy, txz, tyz = gs * sxy, gs * sxz, gs * syz
+            tw = xYZ + yXZ + zXY
+            fxYZ, fyXZ, fzXY = gt * (xYZ + tw), gt * (yXZ + tw), gt * (zXY + tw)
+            fyYZ, fxXZ = gb * yYZ + gc * xXZ, gb * xXZ + gc * yYZ
+            fzYZ, fxXY = gb * zYZ + gc * xXY, gb * xXY + gc * zYZ
+            fyXY, fzXZ = gb * yXY + gc * zXZ, gb * zXZ + gc * yXY
+            FD = [
+                fxX, fxXY, fxXZ, g3 * xXYZ,
+                txy, fyXY, fyXZ, g3 * yXYZ,
+                txz, fzXY, fzXZ, g3 * zXYZ,
+            ]
+            FS = [
+                None, txy, txz, fxYZ,
+                None, fyY, tyz, fyYZ,
+                None, tyz, fzZ, fzYZ,
+            ]
+            lows = [(-FD[m]) if FS[m] is None else FS[m] - FD[m] for m in range(12)]
+            highs = [FD[m] if FS[m] is None else FS[m] + FD[m] for m in range(12)]
+            return lows, highs
+
         def step(chunk, carry):
             r = pl.ds(pl.multiple_of(chunk * 8, 8), 8)
             low = [modes[m, 0, r, :] for m in range(12)]
-            held = [None] * 12
-            for p in range(nx):
-                acc = held
-                if p < nx - 1:
-                    high = [modes[m, p + 1, r, :] for m in range(12)]
-                    S = [low[m] + high[m] if m % 4 else None for m in range(12)]
-                    D = [high[m] - low[m] for m in range(12)]
-                    g = stiff[p, r, :]
-                    xX, xXY, xXZ, xXYZ = D[0:4]
-                    yX, yXY, yXZ, yXYZ = D[4:8]
-                    zX, zXY, zXZ, zXYZ = D[8:12]
-                    _, xY, xZ, xYZ = S[0:4]
-                    _, yY, yZ, yYZ = S[4:8]
-                    _, zY, zZ, zYZ = S[8:12]
-                    div = xX + yY + zZ
-                    sxy, sxz, syz = xY + yX, xZ + zX, yZ + zY
-                    if with_energy:
-                        trace = 0.25 * div
-                        tens = jnp.maximum(trace, 0.0)
-                        third = trace / 3.0
-                        ex, ey, ez = 0.25 * xX - third, 0.25 * yY - third, 0.25 * zZ - third
-                        dev = ex * ex + ey * ey + ez * ez
-                        she = (sxy * sxy + sxz * sxz + syz * syz) * 0.0625
-                        energy = 0.5 * BULK_MODULUS * tens * tens + LAME_MU * (dev + 0.5 * she)
-                        hist[p, r, :] = jnp.where(g > 0.0, energy, 0.0)
-                    gl, g2, gs = k_lame * g, k_two * g, k_shear * g
-                    gt, gb, gc, g3 = k_twist * g, k_bend * g, k_cross * g, k_last * g
-                    pressure = gl * div
-                    fxX, fyY, fzZ = pressure + g2 * xX, pressure + g2 * yY, pressure + g2 * zZ
-                    txy, txz, tyz = gs * sxy, gs * sxz, gs * syz
-                    tw = xYZ + yXZ + zXY
-                    fxYZ, fyXZ, fzXY = gt * (xYZ + tw), gt * (yXZ + tw), gt * (zXY + tw)
-                    fyYZ, fxXZ = gb * yYZ + gc * xXZ, gb * xXZ + gc * yYZ
-                    fzYZ, fxXY = gb * zYZ + gc * xXY, gb * xXY + gc * zYZ
-                    fyXY, fzXZ = gb * yXY + gc * zXZ, gb * zXZ + gc * yXY
-                    FD = [
-                        fxX, fxXY, fxXZ, g3 * xXYZ,
-                        txy, fyXY, fyXZ, g3 * yXYZ,
-                        txz, fzXY, fzXZ, g3 * zXYZ,
-                    ]
-                    FS = [
-                        None, txy, txz, fxYZ,
-                        None, fyY, tyz, fyYZ,
-                        None, tyz, fzZ, fzYZ,
-                    ]
-                    acc = [(-FD[m]) if FS[m] is None else FS[m] - FD[m] for m in range(12)]
-                    if p:
-                        acc = [acc[m] + held[m] for m in range(12)]
-                    held = [FD[m] if FS[m] is None else FS[m] + FD[m] for m in range(12)]
-                    low = high
+            held = None
+            for p in range(nx - 1):
+                high = [modes[m, p + 1, r, :] for m in range(12)]
+                lows, highs = element(low, high, stiff[p, r, :], p, r)
                 for m in range(12):
-                    modes[m, p, r, :] = acc[m]
+                    modes[m, p, r, :] = lows[m] + held[m] if p else lows[m]
+                held, low = highs, high
+            for m in range(12):
+                modes[m, nx - 1, r, :] = held[m]
+            low = [modes[m, GZ, r, :] for m in range(12)]
+            lows, highs = element(low, [x_up(a) for a in low], stiff[GZ, r, :], GZ, r)
+            for m in range(12):
+                modes[m, GZ, r, :] = lows[m] + x_dn(highs[m])
             return carry
 
-        lax.fori_loop(0, rows // 8, step, 0)
-
-    def nodes(c, p):
-        return backward(*(modes[4 * c + m, p] for m in range(4)))
+        lax.fori_loop(0, rows // 8, step, 0, unroll=True)
+
+    def each_node(number, emit, carry):
+        ghosts = [half_back(*(modes[4 * c + m, GZ] for m in range(4))) for c in range(number)]
+
+        def step(p, state):
+            taken, carry = state
+            new, values = [], []
+            for c in range(number):
+                near, far = half_back(*(modes[4 * c + m, p] for m in range(4)))
+                values.append(near + z_dn(far, ghosts[c][1], p))
+                new.append(z_dn_take(taken[c], far, p))
+            return tuple(new), emit(p, values, carry, True)
+
+        first = tuple(pltpu.roll(g[1], 1, 1) for g in ghosts)
+        taken, carry = lax.fori_loop(0, nx, step, (first, carry), unroll=True)
+        emit(GZ, [ghosts[c][0] + taken[c] for c in range(number)], carry, False)
+        return carry
 
     def fold(a):
         part = a[0:8, 0:128]
@@ -593,26 +684,24 @@
     pass_one(lambda c, p: ext[c, p], 3)
     element_pass(True)
 
-    def start_step(p, carry):
-        dot = carry
+    def start_emit(p, values, dot, main):
         inv = inverse[p]
         for c in range(3):
-            r = ext[3 + c, p] - nodes(c, p)
+            r = ext[3 + c, p] - values[c]
             v = inv * r
             basis[c, p] = v
-            resid[c, p] = r[inner]
-            dot = dot + fold((v * r)[inner])
+            if main:
+                resid[c, p] = r[inner]
+                dot = dot + fold((v * r)[inner])
         return dot
 
-    vector = [lax.fori_loop(0, nx, start_step, zero)]
-    hist[nx - 1] = jnp.zeros((rows, lanes), jnp.float32)
-
-    def hist_step(p, low):
-        here = total8_back(hist[p])
-        hist[p] = jnp.maximum(jnp.abs(ext[7, p]), 0.125 * (low + here))
-        return here
-
-    lax.fori_loop(0, nx, hist_step, jnp.zeros((rows, lanes), jnp.float32))
+    vector = [each_node(3, start_emit, zero)]
+    hist[nx - 1] = blank
+
+    def hist_emit(p, total):
+        react[p] = jnp.maximum(jnp.abs(ext[7, p]), 0.125 * total)
+
+    gather_back(hist, hist_emit)
 
     gram = []
     for k in range(DISP_ITERS):
@@ -620,23 +709,27 @@
         element_pass(False)
         more = k + 1 < DISP_ITERS
 
-        def apply_step(p, carry, k=k, more=more):
+        def apply_emit(p, values, carry, main, k=k, more=more):
             carry = list(carry)
+            if not main and not more:
+                return tuple(carry)
             inv = inverse[p] * (2.0 / SPECTRUM) if more else None
             for c in range(3):
-                w = nodes(c, p)
-                wi = w[inner]
-                for j in range(k + 1):
-                    carry[j] = carry[j] + fold(basis[3 * j + c, p, 0:ly, 0:lz] * wi)
+                w = values[c]
+                if main:
+                    wi = w[inner]
+                    for j in range(k + 1):
+                        carry[j] = carry[j] + fold(basis[3 * j + c, p, 0:ly] * wi)
                 if more:
                     v = inv * w - basis[3 * k + c, p]
                     if k:
-                        v = 2.0 * v - basis[3 * (k - 1) + c, p] + 0.0
+                        v = 2.0 * v - basis[3 * (k - 1) + c, p]
                     basis[3 * (k + 1) + c, p] = v
-                    carry[k + 1] = carry[k + 1] + fold(v[inner] * resid[c, p])
+                    if main:
+                        carry[k + 1] = carry[k + 1] + fold(v[inner] * resid[c, p])
             return tuple(carry)
 
-        got = lax.fori_loop(0, nx, apply_step, (zero,) * (k + 1 + (1 if more else 0)))
+        got = each_node(3, apply_emit, (zero,) * (k + 1 + (1 if more else 0)))
         gram.append(list(got[: k + 1]))
         if more:
             vector.append(got[k + 1])
@@ -644,71 +737,83 @@
     l_one = float(laplace_modes[1, 1]) * TOUGHNESS * LENGTH_SCALE
     l_two = float(laplace_modes[3, 3]) * TOUGHNESS * LENGTH_SCALE
     l_three = float(laplace_modes[7, 7]) * TOUGHNESS * LENGTH_SCALE
-    validrow = ((ypos >= 0) & (ypos <= ngy * ly - 2) & (zpos >= 0) & (zpos <= ngz * lz - 2))
 
     def laplace_pass(load):
-        def prime(p):
-            return forward(load(p))
-
-        def step(p, carry):
-            low, held = carry[:4], carry[4:]
-            high = forward(load(p + 1))
+        pass_one(lambda c, p: load(p), 1)
+
+        def element(low, high, mask):
+            m1, m2, m3 = l_one * mask, l_two * mask, l_three * mask
             D = [high[m] - low[m] for m in range(4)]
-            S = [low[m] + high[m] for m in range(1, 4)]
-            F = [l_one * D[0], l_two * D[1], l_two * D[2], l_three * D[3]]
-            F = [jnp.where(validrow, f, 0.0) for f in F]
-            T = [l_one * S[0], l_one * S[1], l_two * S[2]]
-            T = [jnp.where(validrow, f, 0.0) for f in T]
-            acc = [-F[0], T[0] - F[1], T[1] - F[2], T[2] - F[3]]
+            F = [m1 * D[0], m2 * D[1], m2 * D[2], m3 * D[3]]
+            T = [m1 * (low[1] + high[1]), m1 * (low[2] + high[2]), m2 * (low[3] + high[3])]
+            lows = [-F[0]] + [T[m] - F[m + 1] for m in range(3)]
+            highs = [F[0]] + [T[m] + F[m + 1] for m in range(3)]
+            return lows, highs
+
+        for chunk in range(rows // 8):
+            r = slice(8 * chunk, 8 * chunk + 8)
+            low = [modes[m, 0, r, :] for m in range(4)]
+            held = None
+            for p in range(nx - 1):
+                high = [modes[m, p + 1, r, :] for m in range(4)]
+                lows, highs = element(low, high, valid[r])
+                for m in range(4):
+                    modes[m, p, r, :] = lows[m] + held[m] if p else lows[m]
+                held, low = highs, high
             for m in range(4):
-                modes[m, p] = acc[m] + held[m]
-            return tuple(high) + (F[0], T[0] + F[1], T[1] + F[2], T[2] + F[3])
-
-        blank = jnp.zeros((rows, lanes), jnp.float32)
-        out = lax.fori_loop(0, nx - 1, step, tuple(prime(0)) + (blank,) * 4)
-        for m in range(4):
-            modes[m, nx - 1] = out[4 + m]
-
-    corners = total8_back(valid) * (laplace_diag * TOUGHNESS * LENGTH_SCALE)
+                modes[m, nx - 1, r, :] = held[m]
+            low = [modes[m, GZ, r, :] for m in range(4)]
+            lows, highs = element(low, [x_up(a) for a in low], gvalid[r])
+            for m in range(4):
+                modes[m, GZ, r, :] = lows[m] + x_dn(highs[m])
+
+    spread[...] = jnp.zeros(spread.shape, jnp.float32)
+    for p in range(nx - 1):
+        spread[p] = valid
+    spread[GZ] = gvalid
+
+    def spread_emit(p, total):
+        reaction = TOUGHNESS / LENGTH_SCALE + 2.0 * react[p]
+        dinverse[p] = 1.0 / (total * (laplace_diag * TOUGHNESS * LENGTH_SCALE) + reaction)
+
+    gather_back(spread, spread_emit)
+    laplace_pass(lambda p: ext[6, p])
 
     def reaction_of(p):
-        return TOUGHNESS / LENGTH_SCALE + 2.0 * hist[p]
-
-    def damage_inverse(p):
-        twice = jnp.where((p > 0) & (p < nx - 1), 2.0, 1.0)
-        return 1.0 / (corners * twice + reaction_of(p))
-
-    laplace_pass(lambda p: ext[6, p])
-
-    def dstart(p, dot):
-        d = ext[6, p]
-        r = 2.0 * hist[p] - (nodes(0, p) + reaction_of(p) * d)
-        v = damage_inverse(p) * r
+        return TOUGHNESS / LENGTH_SCALE + 2.0 * react[p]
+
+    def dstart(p, values, dot, main):
+        r = 2.0 * react[p] - (values[0] + reaction_of(p) * ext[6, p])
+        v = dinverse[p] * r
         dbasis[0, p] = v
-        dresid[p] = r[inner]
-        return dot + fold((v * r)[inner])
-
-    dvector = [lax.fori_loop(0, nx, dstart, zero)]
+        if main:
+            dresid[p] = r[inner]
+            dot = dot + fold((v * r)[inner])
+        return dot
+
+    dvector = [each_node(1, dstart, zero)]
     dgram = []
     for k in range(DMG_ITERS):
         laplace_pass(lambda p, k=k: dbasis[k, p])
         more = k + 1 < DMG_ITERS
 
-        def dstep(p, carry, k=k, more=more):
+        def dstep(p, values, carry, main, k=k, more=more):
             carry = list(carry)
             here = dbasis[k, p]
-            w = nodes(0, p) + reaction_of(p) * here
-            for j in range(k + 1):
-                carry[j] = carry[j] + fold((dbasis[j, p] * w)[inner])
+            w = values[0] + reaction_of(p) * here
+            if main:
+                for j in range(k + 1):
+                    carry[j] = carry[j] + fold((dbasis[j, p] * w)[inner])
             if more:
-                v = damage_inverse(p) * w - here
+                v = dinverse[p] * w - here
                 if k:
                     v = 2.0 * v - dbasis[k - 1, p]
                 dbasis[k + 1, p] = v
-                carry[k + 1] = carry[k + 1] + fold(v[inner] * dresid[p])
+                if main:
+                    carry[k + 1] = carry[k + 1] + fold(v[inner] * dresid[p])
             return tuple(carry)
 
-        got = lax.fori_loop(0, nx, dstep, (zero,) * (k + 1 + (1 if more else 0)))
+        got = each_node(1, dstep, (zero,) * (k + 1 + (1 if more else 0)))
         dgram.append(list(got[: k + 1]))
         if more:
             dvector.append(got[k + 1])
@@ -732,7 +837,7 @@
     for s in sends:
         s.start()
     for p in range(lx):
-        out_history[p] = hist[xo + p, 0:ly, 0:lz]
+        out_history[p] = react[xo + p, 0:ly]
     for o in range(1, npeer):
         peer_copy(o, lax.rem(me + npeer - o, npeer)).wait_recv()
     whole = sums[0]
@@ -782,8 +887,8 @@
             d = d + dweights[k] * dbasis[k, xo + p, 0:ly, 0:lz]
         out_damage[p] = d
 
-    pl.when(has_down)(y_down.wait_send)
-    pl.when(has_up)(y_up.wait_send)
+    pl.when(has_down)(send_down.wait_send)
+    pl.when(has_up)(send_up.wait_send)
     pl.when(has_left)(z_left.wait_send)
     pl.when(has_right)(z_right.wait_send)
     x_own.wait_send()
@@ -793,16 +898,21 @@
         s.wait_send()
 
 
+def hand_on(*refs):
+    for source, target in zip(refs[:3], refs[3:]):
+        target[...] = source[...]
+
+
 def body_fused(sizes, *arrays):
     ngy, ngz, lx, ly, lz = sizes
-    nx, rows, lanes, fields = 2 * lx, ly + 2 * DEPTH, lz + 128, 8
+    nx, rows, fields = 2 * lx, ly + 2 * DEPTH, 8
     packs = fields * lx // 16
     npeer = ngy * ngz
     f32 = jnp.float32
-    wide = (nx, rows, lanes)
+    wide = (nx + 1, rows, lz)
     vmem = pl.BlockSpec(memory_space=pltpu.VMEM)
     dma = pltpu.SemaphoreType.DMA
-    return pl.pallas_call(
+    results = pl.pallas_call(
         functools.partial(kernel, sizes),
         out_shape=(
             jax.ShapeDtypeStruct((3, lx, ly, lz), f32),
@@ -816,6 +926,9 @@
             pltpu.VMEM((12,) + wide, f32),
             pltpu.VMEM((3 * DISP_ITERS,) + wide, f32),
             pltpu.VMEM((3, nx, ly, lz), f32),
+            pltpu.VMEM(wide, f32),
+            pltpu.VMEM(wide, f32),
+            pltpu.VMEM(wide, f32),
             pltpu.VMEM(wide, f32),
             pltpu.VMEM(wide, f32),
             pltpu.VMEM(wide, f32),
@@ -838,6 +951,12 @@
             collective_id=0, has_side_effects=True, vmem_limit_bytes=60 * 1024 * 1024
         ),
     )(*arrays)
+    return pl.pallas_call(
+        hand_on,
+        out_shape=tuple(jax.ShapeDtypeStruct(r.shape, f32) for r in results),
+        in_specs=[vmem] * 3,
+        out_specs=(vmem,) * 3,
+    )(*results)
 
 
 def solution(mesh):
@@ -846,7 +965,7 @@
     def body(*arrays):
         lx, ly, lz = arrays[2].shape
         fits = shape["gx"] == 2 and shape["gy"] * shape["gz"] > 1
-        fits = fits and lx % 2 == 0 and ly % 8 == 0 and lz == 128
+        fits = fits and lx == 4 and ly % 8 == 0 and lz == 128
         if fits:
             return body_fused((shape["gy"], shape["gz"], lx, ly, lz), *arrays)
         return body_any_mesh(*arrays)

time: 49.4 us -> 34.9 us (0.71)
  Pallas kernels: 45.6 us -> 34.1 us
  local copies, waits for them, and re-layouts: 2.93 us -> 0 us
    pallas_call x1, Pallas kernels: 45.6 us -> 32.5 us  [body_fused(): pl.pallas_call(functools.partial(kernel, sizes), out_shape=(jax.ShapeDtyp...]
    unnamed x7 -> x0, local copies, waits for them, and re-layouts: 2.93 us -> none
    pallas_call x0 -> x1, Pallas kernels: none -> 1.58 us  [body_fused(): pl.pallas_call(hand_on, out_shape=tuple((jax.ShapeDtypeStruct(r.shape, f3...]
where the time goes in v1:
time: 34.9 us; the launch traced here: 34.7 us
  Pallas kernels  34.1 us (98%)
  between operations  0.64 us (2%)
    pallas_call x1, Pallas kernels, body_fused(): pl.pallas_call(functools.partial(kernel, sizes), out_shape=(jax.ShapeDtyp...  32.5 us
    pallas_call x1, Pallas kernels, body_fused(): pl.pallas_call(hand_on, out_shape=tuple((jax.ShapeDtypeStruct(r.shape, f3...  1.58 us

profile of v1, /device:TPU:0, one launch (start us, length us, event | category | flops | bytes accessed | tf_op | source)
XLA Modules:
  0.0 34.7 jit_solution(6072181140952221561)
XLA Ops:
  0.6 32.5 %shard_map.85 = (f32[3,4,16,128]{3,2,1,0:T(8,128)}, f32[4,16,128]{2,1,0:T(8,128)}, f32[4,16,128]{2,1,0:T(8,128)}) custom-call(f32[3,4,16,128]{3,2,1,0:T(8,128)} %disp_ref.1, f32[3,4,16,128]{3,2,1,0:T(8,128)} %force_ref.1, f32[4,16,128]{2,1,0:T(8,128)} %damage_ref.1, f32[4,16,128]{2,1,0:T(8,128)} %history_ref.1, s32[4,16,128]{2,1,0:T(8,128)} %labels_ref.1, ...), custom_call_target="tpu_custom_call" | custom-call | tf_op jit(solution)/shard_map/pallas_call | solution.py:915
  33.2 1.6 %shard_map.86 = (f32[3,4,16,128]{3,2,1,0:T(8,128)}, f32[4,16,128]{2,1,0:T(8,128)}, f32[4,16,128]{2,1,0:T(8,128)}) custom-call(f32[3,4,16,128]{3,2,1,0:T(8,128)} %get-tuple-element.6.refs_0_, f32[4,16,128]{2,1,0:T(8,128)} %get-tuple-element.7.refs_1_, f32[4,16,128]{2,1,0:T(8,128)} %get-tuple-element.8.refs_2_), custom_call_target="tpu_custom_call" | custom-call | tf_op jit(solution)/shard_map/pallas_call | solution.py:954
